TPU v7x, 256 devices: a whole 4x4x8 slice. The times are simulated.
256 devices in a mesh: row: 16 (over z, core), col: 8 (over y_hi, x), depth: 2 (over y_lo).
Axes of the slice: x: 4, y: 4 (y_hi: 2, y_lo: 2; y = y_hi * 2 + y_lo), z: 8, core: 2. Of those that a mesh axis runs over, the one named last changes fastest.
Arguments:
- a_blocks: float32 [32, 32, 256, 256], P('row', ('depth', 'col')), may hold values from -6 to 6
- a_pattern: int32 [32, 32], P('row', ('depth', 'col')), may hold values from 0 to 1, as said below
- b_blocks: float32 [32, 32, 256, 256], P(('depth', 'row'), 'col'), may hold values from -0.125 to 0.125
- b_pattern: int32 [32, 32], P(('depth', 'row'), 'col'), may hold values from 0 to 1, as said below
- c_pattern: int32 [32, 32], P(('row', 'depth'), 'col'), may hold values 0 or 1
Outputs:
- c_blocks: float32 [32, 32, 256, 256], P(('row', 'depth'), 'col')
Inputs may be any that keep to these rules, and one draw needn't show every extreme that they name: Each block row of a_pattern holds between 1 and 8 stored blocks, and some block row holds exactly 8. Each block column of b_pattern holds between 1 and 8 stored blocks, and some block column holds exactly 8.
All inputs are finite; a program needn't handle non-finite values. No bound on the sum of `c_pattern` on one device may be relied on, other than what follows from the above.
Results may differ from a plain program's by a relative error of at most 0.000071.
Values sent between devices are 32-bit elements; how exact they have to be, the bound alone decides.
A program may use at most 128 MiB of HBM per device.

v0:
```python
import jax
import jax.numpy as jnp
from jax import lax
from jax.sharding import PartitionSpec as P


def local(a_blocks, a_pattern, b_blocks, b_pattern, c_pattern):
    left = a_blocks * a_pattern[:, :, None, None].astype(jnp.float32)
    right = b_blocks * b_pattern[:, :, None, None].astype(jnp.float32)
    layer_right = lax.all_gather(right, "row", axis=0, tiled=True)
    partial_value = jnp.einsum(
        "rkab,kcbe->rcae",
        lax.all_gather(left, "col", axis=1, tiled=True),
        layer_right,
        precision=lax.Precision.HIGHEST,
    )
    product = lax.psum_scatter(partial_value, "depth", scatter_dimension=0, tiled=True)
    return product * c_pattern[:, :, None, None].astype(jnp.float32)


def solution(mesh):
    in_specs = (
        P("row", ("depth", "col"), None, None),
        P("row", ("depth", "col")),
        P(("depth", "row"), "col", None, None),
        P(("depth", "row"), "col"),
        P(("row", "depth"), "col"),
    )
    out_specs = P(("row", "depth"), "col", None, None)
    return jax.shard_map(local, mesh=mesh, in_specs=in_specs, out_specs=out_specs, check_vma=False)
```

profile of v0, /device:TPU:1, one launch (start us, length us, event | category | flops | bytes accessed | tf_op | source)
XLA Modules:
  0.0 337.4 jit_solution(12604116690690265737)
XLA Ops:
  6.5 0.0 all-gather.5.cloned.1.call-start
  6.5 0.7 convert_element_type.28
  7.2 2.3 broadcast_multiply_fusion
  9.6 0.0 all-gather.5.cloned.1.call-update
  9.6 0.0 all-gather.3.cloned.1.call-start
  9.6 1.6 copy.8
  11.2 0.7 convert_bitcast_fusion.1
  11.9 1.2 broadcast_multiply_fusion.1
  13.1 0.0 all-gather.3.cloned.1.call-update
  13.1 0.0 copy-start.1
  13.1 0.0 copy-start
  13.1 0.0 all-reduce.3.cloned.1.call-start
  13.2 114.2 %all-gather.5.cloned.1.call-done = f32[2,16,256,256]{3,2,1,0:T(8,128)} async-done(((f32[2,2,256,256]{3,2,1,0:T(8,128)}), f32[2,16,256,256]{3,2,1,0:T(8,128)}) %all-gather.5.cloned.1.call-update) | async-done | bytes 8388624 | tf_op jit(solution)/shard_map/all_gather | solution.py:13
  127.4 96.1 %all-gather.3.cloned.1.call-done = f32[16,4,256,256]{2,3,0,1:T(8,128)} async-done(((f32[1,4,256,256]{2,3,0,1:T(8,128)}), f32[16,4,256,256]{2,3,0,1:T(8,128)}) %all-gather.3.cloned.1.call-update) | async-done | bytes 16777232 | tf_op jit(solution)/shard_map/all_gather | solution.py:10
  223.5 31.1 %fusion.3 = f32[2,4,256,256]{2,3,0,1:T(8,128)} fusion(f32[2,16,256,256]{3,2,1,0:T(8,128)} %all-gather.5.cloned.1.call-done, f32[16,4,256,256]{2,3,0,1:T(8,128)} %all-gather.3.cloned.1.call-done), kind=kOutput, calls=%fused_computation.3 | convolution fusion | flops 25769803776 | bytes 27262976 | tf_op jit(solution)/shard_map/rkab,kcbe->rcae/dot_general | solution.py:11
  254.6 0.0 all-reduce.3.cloned.1.call-update
  254.6 0.0 copy-done.1
  254.6 0.6 dynamic-slice
  255.2 0.0 copy-done
  255.2 72.3 %all-reduce.3.cloned.1.call-done = f32[2,4,256,256]{2,3,0,1:T(8,128)} async-done(((f32[2,4,256,256]{2,3,0,1:T(8,128)}), f32[2,4,256,256]{2,3,0,1:T(8,128)}) %all-reduce.3.cloned.1.call-update) | async-done | bytes 2097168
  327.6 2.0 dynamic-slice_multiply_fusion
  329.6 1.3 copy.9
  (1 shorter events, 0.0 us)
Async XLA Ops:
  6.5 120.8 %all-gather.5.cloned.1.call-start = ((), (), s32[]{:S(2)}) async-start(), calls=%async_computation.1 | async-start | bytes 9437184 | tf_op jit(solution)/shard_map/all_gather | solution.py:13
  9.6 213.9 %all-gather.3.cloned.1.call-start = ((), (), s32[]{:S(2)}) async-start(), calls=%async_computation | async-start | bytes 17825792 | tf_op jit(solution)/shard_map/all_gather | solution.py:10
  13.1 241.5 %copy-start.1 = (u32[256]{0:T(256)S(1)}, u32[256]{0:T(256)}, u32[]{:S(2)}) copy-start(u32[256]{0:T(256)} %constant.7) | copy-start | bytes 3076
  13.1 242.1 %copy-start = (s32[1,4]{1,0:T(1,128)S(1)}, s32[1,4]{1,0:T(1,128)}, u32[]{:S(2)}) copy-start(s32[1,4]{1,0:T(1,128)} %param.9) | copy-start | bytes 52
  13.1 314.4 %all-reduce.3.cloned.1.call-start = ((), (), s32[]{:S(2)}) async-start(), calls=%async_computation.2 | async-start | bytes 4194304
Sparse Core Ops, SparseCore 0:
  10.0 117.3 all-gather.4
  129.2 94.1 all-gather.2
  254.7 72.7 all-reduce.2
where the time goes:
time: 338 us; the launch traced here: 337 us
  waiting for transfers between devices  283 us (84%)
  matrix products  31.1 us (9%)
  between operations  13.2 us (4%)
  other arithmetic  6.93 us (2%)
  local copies, waits for them, and re-layouts  3.46 us (1%)
    all_gather x1, waiting for transfers between devices, local(): lax.all_gather(left, 'col', axis=1, tiled=True)  114 us
    all_gather x1, waiting for transfers between devices, local(): layer_right = lax.all_gather(right, 'row', axis=0, tiled=True)  96.1 us
    unnamed x4, waiting for transfers between devices  72.4 us
    dot_general x1, matrix products, local(): jnp.einsum('rkab,kcbe->rcae', lax.all_gather(left, 'col', axis=1, tiled=T...  31.1 us
  transfers between devices with their start and end apart: 3, of which 3 were waited for; matrix products, arithmetic and copies ran while one was open for 1% of the time, Pallas kernels for 0%

commit v1 on v0

--- a/solution.py
+++ b/solution.py
@@ -4,10 +4,31 @@
 from jax.sharding import PartitionSpec as P
 
 
+def gather_around(x, axis, dim):
+    size, position, width = (lax.axis_size(axis), lax.axis_index(axis), x.shape[dim])
+    right = [(i, (i + 1) % size) for i in range(size)]
+    left = [(i, (i - 1) % size) for i in range(size)]
+    out = jnp.zeros((*x.shape[:dim], size * width, *x.shape[dim + 1 :]), x.dtype)
+    out = lax.dynamic_update_slice_in_dim(out, x, position * width, axis=dim)
+    from_left = from_right = x
+    halfway = size // 2
+    for turn in range(1, halfway + 1):
+        from_left = lax.ppermute(from_left, axis, right)
+        out = lax.dynamic_update_slice_in_dim(
+            out, from_left, (position - turn) % size * width, axis=dim
+        )
+        if turn < size - halfway:
+            from_right = lax.ppermute(from_right, axis, left)
+            out = lax.dynamic_update_slice_in_dim(
+                out, from_right, (position + turn) % size * width, axis=dim
+            )
+    return out
+
+
 def local(a_blocks, a_pattern, b_blocks, b_pattern, c_pattern):
     left = a_blocks * a_pattern[:, :, None, None].astype(jnp.float32)
     right = b_blocks * b_pattern[:, :, None, None].astype(jnp.float32)
-    layer_right = lax.all_gather(right, "row", axis=0, tiled=True)
+    layer_right = gather_around(right, "row", 0)
     partial_value = jnp.einsum(
         "rkab,kcbe->rcae",
         lax.all_gather(left, "col", axis=1, tiled=True),

time: 338 us -> 276 us (0.82)
  waiting for transfers between devices: 283 us -> 130 us
  local copies, waits for them, and re-layouts: 3.46 us -> 48.6 us
  starting transfers between devices: 0.09 us -> 44.5 us
    all_gather x1, waiting for transfers between devices: 114 us -> 0.01 us  [local(): lax.all_gather(left, 'col', axis=1, tiled=True)]
    all_gather x1 -> x0, waiting for transfers between devices: 96.1 us -> none  [local(): layer_right = lax.all_gather(right, 'row', axis=0, tiled=True)]
    ppermute x0 -> x15, waiting for transfers between devices: none -> 52.3 us  [the longest x8 47.5 us: gather_around(): from_left = lax.ppermute(from_left, axis, right)]
    ppermute x0 -> x15, starting transfers between devices: none -> 44.4 us  [the longest x7 26.4 us: gather_around(): from_right = lax.ppermute(from_right, axis, left)]
    ppermute x0 -> x15, local copies, waits for them, and re-layouts: none -> 22.2 us  [the longest x8 11.2 us: gather_around(): from_left = lax.ppermute(from_left, axis, right)]
    dynamic_update_slice x0 -> x16, local copies, waits for them, and re-layouts: none -> 16.3 us  [the longest x8 8.2 us: gather_around(): lax.dynamic_update_slice_in_dim(out, from_left, (position - turn) % size...]
    broadcast_in_dim x0 -> x1, local copies, waits for them, and re-layouts: none -> 7.79 us  [gather_around(): out = jnp.zeros((*x.shape[:dim], size * width, *x.shape[dim + 1:]), x.dtype)]
    unnamed x4 -> x3, waiting for transfers between devices: 72.4 us -> 77.3 us
  transfers between devices with their start and end apart: 3 -> 17, of which waited for: 3 -> 12; matrix products, arithmetic and copies ran while one was open for 1% -> 18% of each run, Pallas kernels for 0% -> 0%
where the time goes in v1:
time: 276 us; the launch traced here: 275 us
  waiting for transfers between devices  130 us (47%)
  local copies, waits for them, and re-layouts  48.6 us (18%)
  starting transfers between devices  44.5 us (16%)
  matrix products  31.3 us (11%)
  between operations  13.9 us (5%)
  other arithmetic  7.1 us (3%)
    unnamed x3, waiting for transfers between devices  77.3 us
    ppermute x8, waiting for transfers between devices, gather_around(): from_left = lax.ppermute(from_left, axis, right)  47.5 us
    dot_general x1, matrix products, local(): jnp.einsum('rkab,kcbe->rcae', lax.all_gather(left, 'col', axis=1, tiled=T...  31.3 us
    ppermute x7, starting transfers between devices, gather_around(): from_right = lax.ppermute(from_right, axis, left)  26.4 us
    ppermute x8, starting transfers between devices, gather_around(): from_left = lax.ppermute(from_left, axis, right)  18 us
    ppermute x8, local copies, waits for them, and re-layouts, gather_around(): from_left = lax.ppermute(from_left, axis, right)  11.2 us
    ppermute x7, local copies, waits for them, and re-layouts, gather_around(): from_right = lax.ppermute(from_right, axis, left)  11 us
    dynamic_update_slice x8, local copies, waits for them, and re-layouts, gather_around(): lax.dynamic_update_slice_in_dim(out, from_left, (position - turn) % size...  8.2 us
  transfers between devices with their start and end apart: 17, of which 12 were waited for; matrix products, arithmetic and copies ran while one was open for 18% of the time, Pallas kernels for 0%

profile of v1, /device:TPU:1, one launch (start us, length us, event | category | flops | bytes accessed | tf_op | source)
XLA Modules:
  0.0 274.9 jit_solution(13892822796453354971)
XLA Ops:
  7.2 2.3 broadcast_multiply_fusion
  10.3 1.4 broadcast_multiply_fusion.1
  11.7 3.0 %collective-permute-start = (f32[1,4,256,256]{3,2,1,0:T(8,128)S(1)}, f32[1,4,256,256]{3,2,1,0:T(8,128)S(1)}, u32[]{:S(2)}, u32[]{:S(2)}) collective-permute-start(f32[1,4,256,256]{3,2,1,0:T(8,128)S(1)} %broadcast_multiply_fusion.1), channel_id=1, source_target_pairs={{0,16},{16,32},{32,48},{48,64},{64,80},{80,96},{96,112},{112,128},... | collective-permute-start | bytes 3145736 | tf_op jit(solution)/shard_map/ppermute | solution.py:16
  15.0 11.5 %collective-permute-done = f32[1,4,256,256]{3,2,1,0:T(8,128)S(1)} collective-permute-done((f32[1,4,256,256]{3,2,1,0:T(8,128)S(1)}, f32[1,4,256,256]{3,2,1,0:T(8,128)S(1)}, u32[]{:S(2)}, u32[]{:S(2)}) %collective-permute-start) | collective-permute-done | bytes 1048608 | tf_op jit(solution)/shard_map/ppermute | solution.py:16
  26.5 2.5 collective-permute-start.2
  29.2 1.8 collective-permute-start.3
  31.0 9.7 %collective-permute-done.2 = f32[1,4,256,256]{3,2,1,0:T(8,128)S(1)} collective-permute-done((f32[1,4,256,256]{3,2,1,0:T(8,128)S(1)}, f32[1,4,256,256]{3,2,1,0:T(8,128)S(1)}, u32[]{:S(2)}, u32[]{:S(2)}) %collective-permute-start.2) | collective-permute-done | bytes 1048608 | tf_op jit(solution)/shard_map/ppermute | solution.py:16
  40.7 2.5 collective-permute-start.4
  43.8 2.7 collective-permute-start.5
  46.5 8.5 %collective-permute-done.4 = f32[1,4,256,256]{3,2,1,0:T(8,128)S(1)} collective-permute-done((f32[1,4,256,256]{3,2,1,0:T(8,128)S(1)}, f32[1,4,256,256]{3,2,1,0:T(8,128)S(1)}, u32[]{:S(2)}, u32[]{:S(2)}) %collective-permute-start.4) | collective-permute-done | bytes 1048608 | tf_op jit(solution)/shard_map/ppermute | solution.py:16
  54.9 2.5 collective-permute-start.6
  58.3 3.6 %collective-permute-start.7 = (f32[1,4,256,256]{3,2,1,0:T(8,128)S(1)}, f32[1,4,256,256]{3,2,1,0:T(8,128)S(1)}, u32[]{:S(2)}, u32[]{:S(2)}) collective-permute-start(f32[1,4,256,256]{3,2,1,0:T(8,128)S(1)} %collective-permute-done.5), channel_id=1, source_target_pairs={{0,240},{16,0},{32,16},{48,32},{64,48},{80,64},{96,80},{112,96},{1... | collective-permute-start | bytes 3145736 | tf_op jit(solution)/shard_map/ppermute | solution.py:21
  61.9 7.2 %collective-permute-done.6 = f32[1,4,256,256]{3,2,1,0:T(8,128)S(1)} collective-permute-done((f32[1,4,256,256]{3,2,1,0:T(8,128)S(1)}, f32[1,4,256,256]{3,2,1,0:T(8,128)S(1)}, u32[]{:S(2)}, u32[]{:S(2)}) %collective-permute-start.6) | collective-permute-done | bytes 1048608 | tf_op jit(solution)/shard_map/ppermute | solution.py:16
  69.2 2.5 collective-permute-start.8
  71.6 1.3 collective-permute-done.7
  72.9 4.4 %collective-permute-start.9 = (f32[1,4,256,256]{3,2,1,0:T(8,128)S(1)}, f32[1,4,256,256]{3,2,1,0:T(8,128)}, u32[]{:S(2)}, u32[]{:S(2)}) collective-permute-start(f32[1,4,256,256]{3,2,1,0:T(8,128)S(1)} %collective-permute-done.7), channel_id=1, source_target_pairs={{0,240},{16,0},{32,16},{48,32},{64,48},{80,64},{96,80},{112,96},{1... | collective-permute-start | bytes 3145736 | tf_op jit(solution)/shard_map/ppermute | solution.py:21
  77.3 6.0 %collective-permute-done.8 = f32[1,4,256,256]{3,2,1,0:T(8,128)S(1)} collective-permute-done((f32[1,4,256,256]{3,2,1,0:T(8,128)S(1)}, f32[1,4,256,256]{3,2,1,0:T(8,128)S(1)}, u32[]{:S(2)}, u32[]{:S(2)}) %collective-permute-start.8) | collective-permute-done | bytes 1048608 | tf_op jit(solution)/shard_map/ppermute | solution.py:16
  83.4 2.5 collective-permute-start.10
  85.9 1.7 collective-permute-done.9
  87.5 5.5 %collective-permute-start.11 = (f32[1,4,256,256]{3,2,1,0:T(8,128)}, f32[1,4,256,256]{3,2,1,0:T(8,128)}, u32[]{:S(2)}, u32[]{:S(2)}) collective-permute-start(f32[1,4,256,256]{3,2,1,0:T(8,128)} %collective-permute-done.9), channel_id=1, source_target_pairs={{0,240},{16,0},{32,16},{48,32},{64,48},{80,64},{96,80},{112,96},{1... | collective-permute-start | bytes 3145736 | tf_op jit(solution)/shard_map/ppermute | solution.py:21
  93.0 4.6 %collective-permute-done.10 = f32[1,4,256,256]{3,2,1,0:T(8,128)} collective-permute-done((f32[1,4,256,256]{3,2,1,0:T(8,128)S(1)}, f32[1,4,256,256]{3,2,1,0:T(8,128)}, u32[]{:S(2)}, u32[]{:S(2)}) %collective-permute-start.10) | collective-permute-done | bytes 1048608 | tf_op jit(solution)/shard_map/ppermute | solution.py:16
  97.6 2.6 collective-permute-start.12
  100.8 7.8 %broadcast_in_dim.2 = f32[16,4,256,256]{2,3,0,1:T(8,128)} broadcast(f32[]{:T(128)} %constant.87.clone.1), dimensions={} | broadcast | bytes 16777220 | tf_op jit(solution)/shard_map/broadcast_in_dim | solution.py:11
  108.6 1.0 constant_dynamic-update-slice_fusion.15
  109.6 1.6 copy.24
  111.2 1.6 copy.25
  112.8 1.0 constant_dynamic-update-slice_fusion.14
  114.9 1.6 copy.26
  116.4 1.6 copy.27
  118.0 1.0 constant_dynamic-update-slice_fusion.12
  120.1 1.6 copy.28
  121.6 1.6 copy.29
  123.2 8.2 %collective-permute-start.13 = (f32[1,4,256,256]{3,2,1,0:T(8,128)}, f32[1,4,256,256]{3,2,1,0:T(8,128)}, u32[]{:S(2)}, u32[]{:S(2)}) collective-permute-start(f32[1,4,256,256]{3,2,1,0:T(8,128)} %collective-permute-done.11), channel_id=1, source_target_pairs={{0,240},{16,0},{32,16},{48,32},{64,48},{80,64},{96,80},{112,96},{1... | collective-permute-start | bytes 3145736 | tf_op jit(solution)/shard_map/ppermute | solution.py:21
  131.4 1.0 constant_dynamic-update-slice_fusion.10
  133.4 1.6 copy.30
  135.0 1.6 copy.31
  136.6 1.0 constant_dynamic-update-slice_fusion.8
  138.6 1.6 copy.32
  140.2 1.6 copy.33
  141.8 1.0 constant_dynamic-update-slice_fusion.6
  143.8 1.6 copy.34
  145.4 1.6 copy.35
  149.3 1.6 copy.37
  152.9 1.6 copy.38
  155.5 31.3 %fusion.3 = f32[2,4,256,256]{2,3,0,1:T(8,128)} fusion(f32[2,16,256,256]{3,2,1,0:T(8,128)} %all-gather.2.cloned.1.call-done, f32[16,4,256,256]{2,3,0,1:T(8,128)} %constant_dynamic-update-slice_fusion), kind=kOutput, calls=%fused_computation.3 | convolution fusion | flops 25769803776 | bytes 27262976 | tf_op jit(solution)/shard_map/rkab,kcbe->rcae/dot_general | solution.py:32
  187.5 77.2 %all-reduce.3.cloned.1.call-done = f32[2,4,256,256]{2,3,0,1:T(8,128)} async-done(((f32[2,4,256,256]{2,3,0,1:T(8,128)}), f32[2,4,256,256]{2,3,0,1:T(8,128)}) %all-reduce.3.cloned.1.call-update) | async-done | bytes 2097168
  264.7 2.0 dynamic-slice_multiply_fusion
  266.7 1.3 copy.39
  (52 shorter events, 14.9 us)
Async XLA Ops:
  6.5 149.0 %all-gather.2.cloned.1.call-start = ((), (), s32[]{:S(2)}) async-start(), calls=%async_computation | async-start | bytes 9437184 | tf_op jit(solution)/shard_map/all_gather | solution.py:34
  9.6 255.1 %all-reduce.3.cloned.1.call-start = ((), (), s32[]{:S(2)}) async-start(), calls=%async_computation.1 | async-start | bytes 4194304
  11.7 14.8 %collective-permute-start = (f32[1,4,256,256]{3,2,1,0:T(8,128)S(1)}, f32[1,4,256,256]{3,2,1,0:T(8,128)S(1)}, u32[]{:S(2)}, u32[]{:S(2)}) collective-permute-start(f32[1,4,256,256]{3,2,1,0:T(8,128)S(1)} %broadcast_multiply_fusion.1), channel_id=1, source_target_pairs={{0,16},{16,32},{32,48},{48,64},{64,80},{80,96},{96,112},{112,128},... | collective-permute-start | bytes 3145736 | tf_op jit(solution)/shard_map/ppermute | solution.py:16
  14.7 14.5 %collective-permute-start.1 = (f32[1,4,256,256]{3,2,1,0:T(8,128)S(1)}, f32[1,4,256,256]{3,2,1,0:T(8,128)S(1)}, u32[]{:S(2)}, u32[]{:S(2)}) collective-permute-start(f32[1,4,256,256]{3,2,1,0:T(8,128)S(1)} %broadcast_multiply_fusion.1), channel_id=1, source_target_pairs={{0,240},{16,0},{32,16},{48,32},{64,48},{80,64},{96,80},{112,96},{1... | collective-permute-start | bytes 3145736 | tf_op jit(solution)/shard_map/ppermute | solution.py:21
  26.5 20.0 %copy-start.3 = (f32[1,4,256,256]{3,2,1,0:T(8,128)}, f32[1,4,256,256]{3,2,1,0:T(8,128)S(1)}, u32[]{:S(2)}) copy-start(f32[1,4,256,256]{3,2,1,0:T(8,128)S(1)} %collective-permute-done) | copy-start | bytes 3145732
  26.5 14.2 %collective-permute-start.2 = (f32[1,4,256,256]{3,2,1,0:T(8,128)S(1)}, f32[1,4,256,256]{3,2,1,0:T(8,128)S(1)}, u32[]{:S(2)}, u32[]{:S(2)}) collective-permute-start(f32[1,4,256,256]{3,2,1,0:T(8,128)S(1)} %collective-permute-done), channel_id=1, source_target_pairs={{0,16},{16,32},{32,48},{48,64},{64,80},{80,96},{96,112},{112,128},... | collective-permute-start | bytes 3145736 | tf_op jit(solution)/shard_map/ppermute | solution.py:16
  29.2 28.2 %copy-start.6 = (f32[1,4,256,256]{3,2,1,0:T(8,128)}, f32[1,4,256,256]{3,2,1,0:T(8,128)S(1)}, u32[]{:S(2)}) copy-start(f32[1,4,256,256]{3,2,1,0:T(8,128)S(1)} %collective-permute-done.1) | copy-start | bytes 3145732
  29.2 14.5 %collective-permute-start.3 = (f32[1,4,256,256]{3,2,1,0:T(8,128)S(1)}, f32[1,4,256,256]{3,2,1,0:T(8,128)S(1)}, u32[]{:S(2)}, u32[]{:S(2)}) collective-permute-start(f32[1,4,256,256]{3,2,1,0:T(8,128)S(1)} %collective-permute-done.1), channel_id=1, source_target_pairs={{0,240},{16,0},{32,16},{48,32},{64,48},{80,64},{96,80},{112,96},{1... | collective-permute-start | bytes 3145736 | tf_op jit(solution)/shard_map/ppermute | solution.py:21
  40.7 21.2 %copy-start.2 = (f32[1,4,256,256]{3,2,1,0:T(8,128)}, f32[1,4,256,256]{3,2,1,0:T(8,128)S(1)}, u32[]{:S(2)}) copy-start(f32[1,4,256,256]{3,2,1,0:T(8,128)S(1)} %collective-permute-done.2) | copy-start | bytes 3145732
  40.7 14.2 %collective-permute-start.4 = (f32[1,4,256,256]{3,2,1,0:T(8,128)S(1)}, f32[1,4,256,256]{3,2,1,0:T(8,128)S(1)}, u32[]{:S(2)}, u32[]{:S(2)}) collective-permute-start(f32[1,4,256,256]{3,2,1,0:T(8,128)S(1)} %collective-permute-done.2), channel_id=1, source_target_pairs={{0,16},{16,32},{32,48},{48,64},{64,80},{80,96},{96,112},{112,128},... | collective-permute-start | bytes 3145736 | tf_op jit(solution)/shard_map/ppermute | solution.py:16
  43.8 56.4 %copy-start.7 = (f32[1,4,256,256]{3,2,1,0:T(8,128)}, f32[1,4,256,256]{3,2,1,0:T(8,128)S(1)}, u32[]{:S(2)}) copy-start(f32[1,4,256,256]{3,2,1,0:T(8,128)S(1)} %collective-permute-done.3) | copy-start | bytes 3145732
  43.8 14.5 %collective-permute-start.5 = (f32[1,4,256,256]{3,2,1,0:T(8,128)S(1)}, f32[1,4,256,256]{3,2,1,0:T(8,128)S(1)}, u32[]{:S(2)}, u32[]{:S(2)}) collective-permute-start(f32[1,4,256,256]{3,2,1,0:T(8,128)S(1)} %collective-permute-done.3), channel_id=1, source_target_pairs={{0,240},{16,0},{32,16},{48,32},{64,48},{80,64},{96,80},{112,96},{1... | collective-permute-start | bytes 3145736 | tf_op jit(solution)/shard_map/ppermute | solution.py:21
  54.9 42.7 %copy-start.4 = (f32[1,4,256,256]{3,2,1,0:T(8,128)}, f32[1,4,256,256]{3,2,1,0:T(8,128)S(1)}, u32[]{:S(2)}) copy-start(f32[1,4,256,256]{3,2,1,0:T(8,128)S(1)} %collective-permute-done.4) | copy-start | bytes 3145732
  54.9 14.2 %collective-permute-start.6 = (f32[1,4,256,256]{3,2,1,0:T(8,128)S(1)}, f32[1,4,256,256]{3,2,1,0:T(8,128)S(1)}, u32[]{:S(2)}, u32[]{:S(2)}) collective-permute-start(f32[1,4,256,256]{3,2,1,0:T(8,128)S(1)} %collective-permute-done.4), channel_id=1, source_target_pairs={{0,16},{16,32},{32,48},{48,64},{64,80},{80,96},{96,112},{112,128},... | collective-permute-start | bytes 3145736 | tf_op jit(solution)/shard_map/ppermute | solution.py:16
  58.3 41.9 %copy-start.8 = (f32[1,4,256,256]{3,2,1,0:T(8,128)}, f32[1,4,256,256]{3,2,1,0:T(8,128)S(1)}, u32[]{:S(2)}) copy-start(f32[1,4,256,256]{3,2,1,0:T(8,128)S(1)} %collective-permute-done.5) | copy-start | bytes 3145732
  58.3 14.6 %collective-permute-start.7 = (f32[1,4,256,256]{3,2,1,0:T(8,128)S(1)}, f32[1,4,256,256]{3,2,1,0:T(8,128)S(1)}, u32[]{:S(2)}, u32[]{:S(2)}) collective-permute-start(f32[1,4,256,256]{3,2,1,0:T(8,128)S(1)} %collective-permute-done.5), channel_id=1, source_target_pairs={{0,240},{16,0},{32,16},{48,32},{64,48},{80,64},{96,80},{112,96},{1... | collective-permute-start | bytes 3145736 | tf_op jit(solution)/shard_map/ppermute | solution.py:21
  69.2 31.1 %copy-start.1 = (f32[1,4,256,256]{3,2,1,0:T(8,128)}, f32[1,4,256,256]{3,2,1,0:T(8,128)S(1)}, u32[]{:S(2)}) copy-start(f32[1,4,256,256]{3,2,1,0:T(8,128)S(1)} %collective-permute-done.6) | copy-start | bytes 3145732
  69.2 14.2 %collective-permute-start.8 = (f32[1,4,256,256]{3,2,1,0:T(8,128)S(1)}, f32[1,4,256,256]{3,2,1,0:T(8,128)S(1)}, u32[]{:S(2)}, u32[]{:S(2)}) collective-permute-start(f32[1,4,256,256]{3,2,1,0:T(8,128)S(1)} %collective-permute-done.6), channel_id=1, source_target_pairs={{0,16},{16,32},{32,48},{48,64},{64,80},{80,96},{96,112},{112,128},... | collective-permute-start | bytes 3145736 | tf_op jit(solution)/shard_map/ppermute | solution.py:16
  72.9 27.3 %copy-start.5 = (f32[1,4,256,256]{3,2,1,0:T(8,128)}, f32[1,4,256,256]{3,2,1,0:T(8,128)S(1)}, u32[]{:S(2)}) copy-start(f32[1,4,256,256]{3,2,1,0:T(8,128)S(1)} %collective-permute-done.7) | copy-start | bytes 3145732
  72.9 14.6 %collective-permute-start.9 = (f32[1,4,256,256]{3,2,1,0:T(8,128)S(1)}, f32[1,4,256,256]{3,2,1,0:T(8,128)}, u32[]{:S(2)}, u32[]{:S(2)}) collective-permute-start(f32[1,4,256,256]{3,2,1,0:T(8,128)S(1)} %collective-permute-done.7), channel_id=1, source_target_pairs={{0,240},{16,0},{32,16},{48,32},{64,48},{80,64},{96,80},{112,96},{1... | collective-permute-start | bytes 3145736 | tf_op jit(solution)/shard_map/ppermute | solution.py:21
  83.4 9.6 %copy-start = (f32[1,4,256,256]{3,2,1,0:T(8,128)}, f32[1,4,256,256]{3,2,1,0:T(8,128)S(1)}, u32[]{:S(2)}) copy-start(f32[1,4,256,256]{3,2,1,0:T(8,128)S(1)} %collective-permute-done.8) | copy-start | bytes 3145732
  83.4 14.2 %collective-permute-start.10 = (f32[1,4,256,256]{3,2,1,0:T(8,128)S(1)}, f32[1,4,256,256]{3,2,1,0:T(8,128)}, u32[]{:S(2)}, u32[]{:S(2)}) collective-permute-start(f32[1,4,256,256]{3,2,1,0:T(8,128)S(1)} %collective-permute-done.8), channel_id=1, source_target_pairs={{0,16},{16,32},{32,48},{48,64},{64,80},{80,96},{96,112},{112,128},... | collective-permute-start | bytes 3145736 | tf_op jit(solution)/shard_map/ppermute | solution.py:16
  87.5 35.7 %collective-permute-start.11 = (f32[1,4,256,256]{3,2,1,0:T(8,128)}, f32[1,4,256,256]{3,2,1,0:T(8,128)}, u32[]{:S(2)}, u32[]{:S(2)}) collective-permute-start(f32[1,4,256,256]{3,2,1,0:T(8,128)} %collective-permute-done.9), channel_id=1, source_target_pairs={{0,240},{16,0},{32,16},{48,32},{64,48},{80,64},{96,80},{112,96},{1... | collective-permute-start | bytes 3145736 | tf_op jit(solution)/shard_map/ppermute | solution.py:21
  97.6 39.0 %collective-permute-start.12 = (f32[1,4,256,256]{3,2,1,0:T(8,128)}, f32[1,4,256,256]{3,2,1,0:T(8,128)S(1)}, u32[]{:S(2)}, u32[]{:S(2)}) collective-permute-start(f32[1,4,256,256]{3,2,1,0:T(8,128)} %collective-permute-done.10), channel_id=1, source_target_pairs={{0,16},{16,32},{32,48},{48,64},{64,80},{80,96},{96,112},{112,128},... | collective-permute-start | bytes 3145736 | tf_op jit(solution)/shard_map/ppermute | solution.py:16
  123.2 26.1 %collective-permute-start.13 = (f32[1,4,256,256]{3,2,1,0:T(8,128)}, f32[1,4,256,256]{3,2,1,0:T(8,128)}, u32[]{:S(2)}, u32[]{:S(2)}) collective-permute-start(f32[1,4,256,256]{3,2,1,0:T(8,128)} %collective-permute-done.11), channel_id=1, source_target_pairs={{0,240},{16,0},{32,16},{48,32},{64,48},{80,64},{96,80},{112,96},{1... | collective-permute-start | bytes 3145736 | tf_op jit(solution)/shard_map/ppermute | solution.py:21
  136.6 16.3 %collective-permute-start.14 = (f32[1,4,256,256]{3,2,1,0:T(8,128)S(1)}, f32[1,4,256,256]{3,2,1,0:T(8,128)}, u32[]{:S(2)}, u32[]{:S(2)}) collective-permute-start(f32[1,4,256,256]{3,2,1,0:T(8,128)S(1)} %collective-permute-done.12), channel_id=1, source_target_pairs={{0,16},{16,32},{32,48},{48,64},{64,80},{80,96},{96,112},{112,128},... | collective-permute-start | bytes 3145736 | tf_op jit(solution)/shard_map/ppermute | solution.py:16
  155.5 31.4 %copy-start.10 = (u32[256]{0:T(256)S(1)}, u32[256]{0:T(256)}, u32[]{:S(2)}) copy-start(u32[256]{0:T(256)} %constant.115) | copy-start | bytes 3076
  155.5 32.0 %copy-start.9 = (s32[1,4]{1,0:T(1,128)S(1)}, s32[1,4]{1,0:T(1,128)}, u32[]{:S(2)}) copy-start(s32[1,4]{1,0:T(1,128)} %param.9) | copy-start | bytes 52
Sparse Core Ops, SparseCore 0:
  10.0 117.3 all-gather.1
  187.0 77.6 all-reduce.2
